TPU v7x, 256 devices: a whole 4x4x8 slice. The times are simulated.
256 devices in a mesh: row: 16 (over z_hi, y, core), col: 16 (over x, z_lo).
Axes of the slice: x: 4, y: 4, z: 8 (z_hi: 2, z_lo: 4; z = z_hi * 4 + z_lo), core: 2. Of those that a mesh axis runs over, the one named last changes fastest.
Arguments:
- cost_rough: bfloat16 [33792, 33792], P('row', 'col'), may hold values from 0.0009994507 to 1
- land_mask: int32 [176, 192], P('row', 'col'), may hold values 0 or 1
- wage_start: float32 [176, 192, 256], P('row', 'col'), may hold values from -3 to 3
- tech_start: float32 [176, 192, 256], P('row', 'col'), may hold values from -3 to 3
- temp_start: float32 [176, 192, 256], P('row', 'col'), may hold values from -2.5 to 2.5
- damping: float32 [1], replicated, may hold values from 0.3 to 0.8
Outputs:
- wage_field: float32 [176, 192, 256], P('row', 'col')
- tech_field: float32 [176, 192, 256], P('row', 'col')
- temp_field: float32 [176, 192, 256], P('row', 'col')
All inputs are finite; a program needn't handle non-finite values. No bound on the sum of `land_mask` on one device may be relied on, other than what follows from the above.
Results may differ from a plain program's by a relative error of at most 0.0003.
Values may be sent and summed in bfloat16 or wider, within the bound.
A program may use at most 128 MiB of HBM per device.

v0:
```python
import jax
import jax.numpy as jnp
from jax import lax
from jax.sharding import PartitionSpec as P

LAT = 176
LON = 192
ITERS = 3
ELL = 44


def padded_2(cells, sides, width):
    for axis, dim in sides:
        count = lax.axis_size(axis)
        ends = count - 1
        head = lax.slice_in_dim(cells, 0, width, axis=dim)
        tail = lax.slice_in_dim(cells, cells.shape[dim] - width, cells.shape[dim], axis=dim)
        cells = jnp.concatenate(
            [
                lax.ppermute(tail, axis, [(i, (i + 1) % count) for i in range(ends)]),
                cells,
                lax.ppermute(head, axis, [((i + 1) % count, i) for i in range(ends)]),
            ],
            axis=dim,
        )
    return cells


def cost_block(rough_block, destin, source):
    distance = (
        jnp.abs(destin[:, None] // LON - source[None, :] % LAT)
        + jnp.abs(destin[:, None] % LON - source[None, :] // LAT)
    ).astype(jnp.float32)
    scaled = rough_block.astype(jnp.float32) * jnp.exp(-distance / ELL) / (ELL * ELL)
    return scaled.astype(jnp.bfloat16)


def laplace(padded, field):
    return padded[2:, 1:-1] + padded[:-2, 1:-1] + padded[1:-1, 2:] + padded[1:-1, :-2] - 4.0 * field


def local(cost_rough, land_mask, wage_start, tech_start, temp_start, damping):
    height, breadth = cost_rough.shape
    band_lat, band_lon, scenarios = wage_start.shape
    source = lax.axis_index("col") * breadth + jnp.arange(breadth, dtype=jnp.int32)
    lat_first = lax.axis_index("row") * band_lat

    def build_row(pair):
        rough_row, lat_offset = pair
        destin = (lat_first + lat_offset) * LON + jnp.arange(LON, dtype=jnp.int32)
        return cost_block(rough_row, destin, source)

    slabs = lax.map(
        build_row,
        (cost_rough.reshape(band_lat, LON, breadth), jnp.arange(band_lat, dtype=jnp.int32)),
    )
    cost_tile = slabs.reshape(height, breadth)
    share = 0.25 + land_mask.astype(jnp.float32)[:, :, None]
    wage_field, tech_field, temp_field = (wage_start, tech_start, temp_start)
    for iteration in range(ITERS):
        supply = (jnp.exp(tech_field - wage_field) * share).astype(jnp.bfloat16)
        gathered = lax.all_gather(supply, "row", axis=0, tiled=True)
        columns = gathered.transpose(1, 0, 2).reshape(breadth, scenarios)
        product = jnp.dot(cost_tile, columns, preferred_element_type=jnp.float32).reshape(
            band_lat, LON, scenarios
        )
        access = lax.psum_scatter(product, "col", scatter_dimension=1, tiled=True)
        target = 0.5 * (jnp.log(access) + tech_field)
        wage_field = wage_field + damping[0] * (target - wage_field)
        stacked = jnp.stack((tech_field, temp_field))
        padded = padded_2(stacked, (("row", 1), ("col", 2)), 1)
        tech_next = (
            tech_field + 0.2 * laplace(padded[0], tech_field) - 0.05 * temp_field * temp_field
        )
        temp_next = (
            temp_field + 0.2 * laplace(padded[1], temp_field) + 0.5 * share * jnp.tanh(wage_field)
        )
        tech_field, temp_field = (tech_next, temp_next)
    return (wage_field, tech_field, temp_field)


def solution(mesh):
    in_specs = (
        P("row", "col"),
        P("row", "col"),
        P("row", "col", None),
        P("row", "col", None),
        P("row", "col", None),
        P(),
    )
    out_specs = (P("row", "col", None), P("row", "col", None), P("row", "col", None))
    return jax.shard_map(local, mesh=mesh, in_specs=in_specs, out_specs=out_specs, check_vma=False)
```

profile of v0, /device:TPU:24, one launch (start us, length us, event | category | flops | bytes accessed | tf_op | source)
XLA Modules:
  0.0 748.9 jit_solution(5490739183297818805)
XLA Ops:
  9.8 47.7 %while.15 = (s32[]{:T(128)}, bf16[11,192,2112]{2,1,0:T(8,128)(2,1)}, bf16[11,192,2112]{2,1,0:T(8,128)(2,1)}, s32[11]{0:T(128)S(1)}, s32[]{:T(128)}, /*index=5*/s32[]{:T(128)}, s32[]{:T(128)}, s32[]{:T(128)}) while((s32[]{:T(128)}, bf16[11,192,2112]{2,1,0:T(8,128)(2,1)}, bf16[11,192,2112]{2,1,0:T(8,128)(2,1)}, ...), condition=%wide.region_1.2_spmd.clone.clone, body=%wide.region_0.1_spmd.clone.clone.sunk | while | flops 4898116 | bytes 1712901 | solution.py:53
  11.0 3.1 fusion.66
  19.7 3.1 fusion.66
  28.3 3.1 fusion.66
  32.6 3.1 fusion.66
  37.0 3.1 fusion.66
  41.3 3.1 fusion.66
  45.6 3.1 fusion.66
  49.9 3.1 fusion.66
  54.3 3.1 fusion.66
  57.4 14.5 %all-gather.4.cloned.1.call-done = bf16[176,12,256]{2,1,0:T(8,128)(2,1)} async-done(((bf16[11,12,256]{2,1,0:T(8,128)(2,1)}), bf16[176,12,256]{2,1,0:T(8,128)(2,1)}) %all-gather.4.cloned.1.call-update) | async-done | bytes 1081360 | tf_op jit(solution)/shard_map/all_gather | solution.py:62
  73.7 7.8 %fusion.56 = f32[11,192,256]{2,1,0:T(8,128)} fusion(bf16[11,192,2112]{2,1,0:T(8,128)(2,1)} %get-tuple-element.124, bf16[2112,256,1]{1,0,2:T(8,128)(2,1)S(1)} %bitcast.73), kind=kOutput, calls=%fused_computation.113 | convolution fusion | flops 2283798528 | bytes 12165120 | tf_op jit(solution)/shard_map/dot_general | solution.py:64
  84.6 3.4 collective-permute-start.1
  97.7 157.4 %all-reduce.7.cloned.1.call-done = f32[11,192,256]{2,1,0:T(8,128)} async-done(((f32[11,192,256]{2,1,0:T(8,128)}), f32[11,192,256]{2,1,0:T(8,128)}) %all-reduce.7.cloned.1.call-update) | async-done | bytes 2162704
  257.1 57.6 %all-gather.6.cloned.1.call-done = bf16[176,12,256]{2,1,0:T(8,128)(2,1)} async-done(((bf16[11,12,256]{2,1,0:T(8,128)(2,1)}), bf16[176,12,256]{2,1,0:T(8,128)(2,1)}) %all-gather.6.cloned.1.call-update) | async-done | bytes 1081360 | tf_op jit(solution)/shard_map/all_gather | solution.py:62
  316.4 7.8 %fusion.57 = f32[11,192,256]{2,1,0:T(8,128)} fusion(bf16[11,192,2112]{2,1,0:T(8,128)(2,1)} %get-tuple-element.124, bf16[2112,256,1]{1,0,2:T(8,128)(2,1)S(1)} %bitcast.75), kind=kOutput, calls=%fused_computation.114 | convolution fusion | flops 2283798528 | bytes 12165120 | tf_op jit(solution)/shard_map/dot_general | solution.py:64
  326.4 3.4 collective-permute-start.5
  334.8 4.6 collective-permute-done.7
  339.6 157.7 %all-reduce.9.cloned.1.call-done = f32[11,192,256]{2,1,0:T(8,128)} async-done(((f32[11,192,256]{2,1,0:T(8,128)}), f32[11,192,256]{2,1,0:T(8,128)}) %all-reduce.9.cloned.1.call-update) | async-done | bytes 2162704
  499.4 57.8 %all-gather.8.cloned.1.call-done = bf16[176,12,256]{2,1,0:T(8,128)(2,1)} async-done(((bf16[11,12,256]{2,1,0:T(8,128)(2,1)}), bf16[176,12,256]{2,1,0:T(8,128)(2,1)}) %all-gather.8.cloned.1.call-update) | async-done | bytes 1081360 | tf_op jit(solution)/shard_map/all_gather | solution.py:62
  558.9 7.7 %fusion.58 = f32[11,192,256]{2,1,0:T(8,128)} fusion(bf16[11,192,2112]{2,1,0:T(8,128)(2,1)} %get-tuple-element.124, bf16[2112,256,1]{1,0,2:T(8,128)(2,1)S(1)} %bitcast.74), kind=kOutput, calls=%fused_computation.115 | convolution fusion | flops 2283798528 | bytes 12165120 | tf_op jit(solution)/shard_map/dot_general | solution.py:64
  568.8 3.4 collective-permute-start.9
  577.2 4.7 collective-permute-done.11
  581.9 158.1 %all-reduce.11.cloned.1.call-done = f32[11,192,256]{2,1,0:T(8,128)} async-done(((f32[11,192,256]{2,1,0:T(8,128)}), f32[11,192,256]{2,1,0:T(8,128)}) %all-reduce.11.cloned.1.call-update) | async-done | bytes 2162704
  (110 shorter events, 53.1 us)
Async XLA Ops:
  7.2 64.8 %all-gather.4.cloned.1.call-start = ((), (), s32[]{:S(2)}) async-start(), calls=%async_computation | async-start | bytes 1531904 | tf_op jit(solution)/shard_map/all_gather | solution.py:62
  9.7 245.4 %all-reduce.7.cloned.1.call-start = ((), (), s32[]{:S(2)}) async-start(), calls=%async_computation.3 | async-start | bytes 4325376
  81.4 0.9 copy-start
  81.4 1.0 copy-start.1
  81.4 12.0 %copy-start.3 = (u32[256]{0:T(256)S(1)}, u32[256]{0:T(256)}, u32[]{:S(2)}) copy-start(u32[256]{0:T(256)} %constant.114) | copy-start | bytes 3076
  81.5 173.7 %copy-start.2 = (f32[11,12,256]{2,1,0:T(8,128)S(1)}, f32[11,12,256]{2,1,0:T(8,128)}, u32[]{:S(2)}) copy-start(f32[11,12,256]{2,1,0:T(8,128)} %param.10) | copy-start | bytes 405508
  81.5 233.2 %all-gather.6.cloned.1.call-start = ((), (), s32[]{:S(2)}) async-start(), calls=%async_computation.1 | async-start | bytes 1531904 | tf_op jit(solution)/shard_map/all_gather | solution.py:62
  82.5 5.6 collective-permute-start
  84.6 5.0 collective-permute-start.1
  89.6 5.0 collective-permute-start.2
  91.5 6.1 collective-permute-start.3
  257.0 240.2 %all-reduce.9.cloned.1.call-start = ((), (), s32[]{:S(2)}) async-start(), calls=%async_computation.4 | async-start | bytes 4325376
  324.2 233.0 %all-gather.8.cloned.1.call-start = ((), (), s32[]{:S(2)}) async-start(), calls=%async_computation.2 | async-start | bytes 1531904 | tf_op jit(solution)/shard_map/all_gather | solution.py:62
  324.3 5.6 collective-permute-start.4
  326.4 5.0 collective-permute-start.5
  331.5 3.3 collective-permute-start.6
  333.3 6.1 collective-permute-start.7
  499.1 240.9 %all-reduce.11.cloned.1.call-start = ((), (), s32[]{:S(2)}) async-start(), calls=%async_computation.5 | async-start | bytes 4325376
  566.6 5.6 collective-permute-start.8
  568.8 5.0 collective-permute-start.9
  573.8 3.3 collective-permute-start.10
  575.6 6.2 collective-permute-start.11
Sparse Core Ops, SparseCore 0:
  11.3 60.6 all-gather.3
  81.6 173.4 all-reduce.6
  258.4 56.2 all-gather.5
  324.3 172.8 all-reduce.8
  500.4 56.7 all-gather.7
  566.7 173.2 all-reduce.10
where the time goes:
time: 750 us; the launch traced here: 749 us
  waiting for transfers between devices  621 us (83%)
  other arithmetic  43.5 us (6%)
  starting transfers between devices  26.4 us (4%)
  matrix products  23.2 us (3%)
  between operations  15.7 us (2%)
  local copies, waits for them, and re-layouts  13.1 us (2%)
    unnamed x9, waiting for transfers between devices  473 us
    all_gather x3, waiting for transfers between devices, local(): gathered = lax.all_gather(supply, 'row', axis=0, tiled=True)  130 us
    dynamic_update_slice x11, other arithmetic, local(): lax.map(build_row, (cost_rough.reshape(band_lat, LON, breadth), jnp.arang...  33.9 us
    dot_general x3, matrix products, local(): jnp.dot(cost_tile, columns, preferred_element_type=jnp.float32)  23.2 us
    ppermute x6, waiting for transfers between devices, padded_2(): lax.ppermute(head, axis, [((i + 1) % count, i) for i in range(ends)])  16.9 us
  transfers between devices with their start and end apart: 18, of which 14 were waited for; matrix products, arithmetic and copies ran while one was open for 6% of the time, Pallas kernels for 0%

commit v1 on v0

--- a/solution.py
+++ b/solution.py
@@ -59,7 +59,10 @@
     wage_field, tech_field, temp_field = (wage_start, tech_start, temp_start)
     for iteration in range(ITERS):
         supply = (jnp.exp(tech_field - wage_field) * share).astype(jnp.bfloat16)
-        gathered = lax.all_gather(supply, "row", axis=0, tiled=True)
+        size = lax.axis_size("row")
+        shards = jnp.stack([supply for _ in range(size)])
+        shards = lax.all_to_all(shards, "row", split_axis=0, concat_axis=0)
+        gathered = jnp.concatenate(shards, axis=0)
         columns = gathered.transpose(1, 0, 2).reshape(breadth, scenarios)
         product = jnp.dot(cost_tile, columns, preferred_element_type=jnp.float32).reshape(
             band_lat, LON, scenarios

time: 750 us -> 721 us (0.961)
  waiting for transfers between devices: 621 us -> 498 us
  blocking collectives: 0 us -> 85.7 us
  starting transfers between devices: 26.4 us -> 37.5 us
    all_gather x3 -> x0, waiting for transfers between devices: 130 us -> none  [local(): gathered = lax.all_gather(supply, 'row', axis=0, tiled=True)]
    all_to_all x0 -> x2, blocking collectives: none -> 85.7 us  [local(): shards = lax.all_to_all(shards, 'row', split_axis=0, concat_axis=0)]
    all_to_all x0 -> x1, starting transfers between devices: none -> 11.3 us  [local(): shards = lax.all_to_all(shards, 'row', split_axis=0, concat_axis=0)]
    ppermute x6, waiting for transfers between devices: 16.9 us -> 27 us  [padded_2(): lax.ppermute(head, axis, [((i + 1) % count, i) for i in range(ends)])]
    unnamed x9 -> x6, waiting for transfers between devices: 473 us -> 471 us
  transfers between devices with their start and end apart: 18 -> 16, of which waited for: 14 -> 11; matrix products, arithmetic and copies ran while one was open for 6% -> 6% of each run, Pallas kernels for 0% -> 0%
where the time goes in v1:
time: 721 us; the launch traced here: 720 us
  waiting for transfers between devices  498 us (69%)
  blocking collectives  85.7 us (12%)
  other arithmetic  41.6 us (6%)
  starting transfers between devices  37.5 us (5%)
  matrix products  23.3 us (3%)
  between operations  15.3 us (2%)
  local copies, waits for them, and re-layouts  10.9 us (2%)
    unnamed x6, waiting for transfers between devices  471 us
    all_to_all x2, blocking collectives, local(): shards = lax.all_to_all(shards, 'row', split_axis=0, concat_axis=0)  85.7 us
    dynamic_update_slice x11, other arithmetic, local(): lax.map(build_row, (cost_rough.reshape(band_lat, LON, breadth), jnp.arang...  33.9 us
    ppermute x6, waiting for transfers between devices, padded_2(): lax.ppermute(head, axis, [((i + 1) % count, i) for i in range(ends)])  27 us
    dot_general x3, matrix products, local(): jnp.dot(cost_tile, columns, preferred_element_type=jnp.float32)  23.3 us
  transfers between devices with their start and end apart: 16, of which 11 were waited for; matrix products, arithmetic and copies ran while one was open for 6% of the time, Pallas kernels for 0%

profile of v1, /device:TPU:24, one launch (start us, length us, event | category | flops | bytes accessed | tf_op | source)
XLA Modules:
  0.0 719.8 jit_solution(5176384223658942896)
XLA Ops:
  10.2 11.3 %all-to-all-start = ((bf16[16,11,12,256]{3,2,1,0:T(8,128)(2,1)}), bf16[16,11,12,256]{3,2,1,0:T(8,128)(2,1)S(1)}, u32[]{:S(2)}, u32[]{:S(2)}) async-start(bf16[16,11,12,256]{3,2,1,0:T(8,128)(2,1)} %stack.24), calls=%async_computation | async-start | bytes 2883584 | tf_op jit(solution)/shard_map/all_to_all | solution.py:64
  21.6 48.9 %while.15 = (s32[]{:T(128)}, bf16[11,192,2112]{2,1,0:T(8,128)(2,1)}, bf16[11,192,2112]{2,1,0:T(8,128)(2,1)}, s32[11]{0:T(128)S(1)}, s32[]{:T(128)}, /*index=5*/s32[]{:T(128)}, s32[]{:T(128)}, s32[]{:T(128)}) while((s32[]{:T(128)}, bf16[11,192,2112]{2,1,0:T(8,128)(2,1)}, bf16[11,192,2112]{2,1,0:T(8,128)(2,1)}, ...), condition=%wide.region_1.2_spmd.clone.clone, body=%wide.region_0.1_spmd.clone.clone.sunk | while | flops 4898116 | bytes 1712901 | solution.py:53
  27.4 3.1 fusion.66
  45.1 3.1 fusion.66
  49.5 3.1 fusion.66
  62.8 3.1 fusion.66
  67.3 3.1 fusion.66
  70.8 7.8 %fusion.56 = f32[11,192,256]{2,1,0:T(8,128)} fusion(bf16[11,192,2112]{2,1,0:T(8,128)(2,1)} %get-tuple-element.124, bf16[2112,256,1]{1,0,2:T(8,128)(2,1)S(1)} %bitcast.79), kind=kOutput, calls=%fused_computation.113 | convolution fusion | flops 2283798528 | bytes 12165120 | tf_op jit(solution)/shard_map/dot_general | solution.py:67
  81.7 3.5 collective-permute-start.1
  85.2 4.4 collective-permute-done.1
  95.8 3.6 collective-permute-done.3
  99.5 157.2 %all-reduce.7.cloned.1.call-done = f32[11,192,256]{2,1,0:T(8,128)} async-done(((f32[11,192,256]{2,1,0:T(8,128)}), f32[11,192,256]{2,1,0:T(8,128)}) %all-reduce.7.cloned.1.call-update) | async-done | bytes 2162704
  258.1 42.7 %all_to_all.15 = bf16[16,11,12,256]{3,2,1,0:T(8,128)(2,1)S(1)} all-to-all(bf16[16,11,12,256]{3,2,1,0:T(8,128)(2,1)S(1)} %stack.28), channel_id=1, replica_groups=mesh['row'=16,'col'=16] {'row'}, dimensions={0} | all-to-all | bytes 2162688 | tf_op jit(solution)/shard_map/all_to_all | solution.py:64
  301.1 7.8 %fusion.57 = f32[11,192,256]{2,1,0:T(8,128)} fusion(bf16[11,192,2112]{2,1,0:T(8,128)(2,1)} %get-tuple-element.124, bf16[2112,256,1]{1,0,2:T(8,128)(2,1)S(1)} %bitcast.81), kind=kOutput, calls=%fused_computation.114 | convolution fusion | flops 2283798528 | bytes 12165120 | tf_op jit(solution)/shard_map/dot_general | solution.py:67
  311.3 3.4 collective-permute-start.5
  314.6 5.2 collective-permute-done.5
  322.6 4.6 collective-permute-done.7
  327.4 156.6 %all-reduce.9.cloned.1.call-done = f32[11,192,256]{2,1,0:T(8,128)} async-done(((f32[11,192,256]{2,1,0:T(8,128)}), f32[11,192,256]{2,1,0:T(8,128)}) %all-reduce.9.cloned.1.call-update) | async-done | bytes 2162704
  485.3 43.0 %all_to_all.16 = bf16[16,11,12,256]{3,2,1,0:T(8,128)(2,1)S(1)} all-to-all(bf16[16,11,12,256]{3,2,1,0:T(8,128)(2,1)S(1)} %stack.32), channel_id=1, replica_groups=mesh['row'=16,'col'=16] {'row'}, dimensions={0} | all-to-all | bytes 2162688 | tf_op jit(solution)/shard_map/all_to_all | solution.py:64
  528.7 7.7 %fusion.58 = f32[11,192,256]{2,1,0:T(8,128)} fusion(bf16[11,192,2112]{2,1,0:T(8,128)(2,1)} %get-tuple-element.124, bf16[2112,256,1]{1,0,2:T(8,128)(2,1)S(1)} %bitcast.80), kind=kOutput, calls=%fused_computation.115 | convolution fusion | flops 2283798528 | bytes 12165120 | tf_op jit(solution)/shard_map/dot_general | solution.py:67
  538.7 3.4 collective-permute-start.9
  542.0 4.8 collective-permute-done.9
  549.7 4.5 collective-permute-done.11
  554.3 157.0 %all-reduce.11.cloned.1.call-done = f32[11,192,256]{2,1,0:T(8,128)} async-done(((f32[11,192,256]{2,1,0:T(8,128)}), f32[11,192,256]{2,1,0:T(8,128)}) %all-reduce.11.cloned.1.call-update) | async-done | bytes 2162704
  (108 shorter events, 53.4 us)
Async XLA Ops:
  10.2 60.3 %all-to-all-start = ((bf16[16,11,12,256]{3,2,1,0:T(8,128)(2,1)}), bf16[16,11,12,256]{3,2,1,0:T(8,128)(2,1)S(1)}, u32[]{:S(2)}, u32[]{:S(2)}) async-start(bf16[16,11,12,256]{3,2,1,0:T(8,128)(2,1)} %stack.24), calls=%async_computation | async-start | bytes 2883584 | tf_op jit(solution)/shard_map/all_to_all | solution.py:64
  21.5 235.2 %all-reduce.7.cloned.1.call-start = ((), (), s32[]{:S(2)}) async-start(), calls=%async_computation.3 | async-start | bytes 4325376
  78.6 0.9 copy-start
  78.6 1.0 copy-start.1
  78.6 15.9 %copy-start.3 = (u32[256]{0:T(256)S(1)}, u32[256]{0:T(256)}, u32[]{:S(2)}) copy-start(u32[256]{0:T(256)} %constant.114) | copy-start | bytes 3076
  78.7 178.1 %copy-start.2 = (f32[11,12,256]{2,1,0:T(8,128)S(1)}, f32[11,12,256]{2,1,0:T(8,128)}, u32[]{:S(2)}) copy-start(f32[11,12,256]{2,1,0:T(8,128)} %param.10) | copy-start | bytes 405508
  78.7 405.3 %all-reduce.9.cloned.1.call-start = ((), (), s32[]{:S(2)}) async-start(), calls=%async_computation.4 | async-start | bytes 4325376
  79.6 5.6 collective-permute-start
  81.7 8.0 %collective-permute-start.1 = (f32[2,1,12,256]{3,2,1,0:T(8,128)S(1)}, f32[2,1,12,256]{3,2,1,0:T(8,128)S(1)}, u32[]{:S(2)}, u32[]{:S(2)}) collective-permute-start(f32[2,1,12,256]{3,2,1,0:T(8,128)S(1)} %get-tuple-element.205), channel_id=1, source_target_pairs={{16,0},{32,16},{48,32},{64,48},{80,64},{96,80},{112,96},{128,112},... | collective-permute-start | bytes 73736 | tf_op jit(solution)/shard_map/ppermute | solution.py:22
  89.7 6.1 collective-permute-start.2
  92.6 6.8 collective-permute-start.3
  309.0 402.3 %all-reduce.11.cloned.1.call-start = ((), (), s32[]{:S(2)}) async-start(), calls=%async_computation.5 | async-start | bytes 4325376
  309.0 5.6 collective-permute-start.4
  311.3 8.5 %collective-permute-start.5 = (f32[2,1,12,256]{3,2,1,0:T(8,128)S(1)}, f32[2,1,12,256]{3,2,1,0:T(8,128)S(1)}, u32[]{:S(2)}, u32[]{:S(2)}) collective-permute-start(f32[2,1,12,256]{3,2,1,0:T(8,128)S(1)} %get-tuple-element.203), channel_id=1, source_target_pairs={{16,0},{32,16},{48,32},{64,48},{80,64},{96,80},{112,96},{128,112},... | collective-permute-start | bytes 73736 | tf_op jit(solution)/shard_map/ppermute | solution.py:22
  319.8 2.8 collective-permute-start.6
  321.1 6.1 collective-permute-start.7
  536.4 5.6 collective-permute-start.8
  538.7 8.2 %collective-permute-start.9 = (f32[2,1,12,256]{3,2,1,0:T(8,128)S(1)}, f32[2,1,12,256]{3,2,1,0:T(8,128)S(1)}, u32[]{:S(2)}, u32[]{:S(2)}) collective-permute-start(f32[2,1,12,256]{3,2,1,0:T(8,128)S(1)} %get-tuple-element.201), channel_id=1, source_target_pairs={{16,0},{32,16},{48,32},{64,48},{80,64},{96,80},{112,96},{128,112},... | collective-permute-start | bytes 73736 | tf_op jit(solution)/shard_map/ppermute | solution.py:22
  546.9 2.8 collective-permute-start.10
  548.2 6.0 collective-permute-start.11
Sparse Core Ops, SparseCore 0:
  78.8 177.9 all-reduce.6
  309.1 174.8 all-reduce.8
  536.5 174.7 all-reduce.10
